TPU v7x, 512 devices: a whole 4x8x8 slice. The times are simulated.
512 devices in a mesh: gx: 32 (over z, y_lo), gy: 16 (over x, y_hi, core).
Axes of the slice: x: 4, y: 8 (y_hi: 2, y_lo: 4; y = y_hi * 4 + y_lo), z: 8, core: 2. Of those that a mesh axis runs over, the one named last changes fastest.
Arguments:
- ensemble: float32 [40, 8, 64, 4096], P(None, None, 'gy', 'gx'), may hold values from 0.2 to 2
- courant_x: float32 [2, 64, 4096], P(None, 'gy', 'gx'), may hold values from -0.4 to 0.4
- courant_y: float32 [2, 64, 4096], P(None, 'gy', 'gx'), may hold values from -0.4 to 0.4
- diffusion: float32 [64, 4096], P('gy', 'gx'), may hold values from 0.02 to 0.12
- mixing: float32 [64, 4096], P('gy', 'gx'), may hold values from 0.02 to 0.2
- growth: float32 [2, 64, 4096], P(None, 'gy', 'gx'), may hold values from 0.05 to 0.5
- land_sea: int32 [64, 4096], P('gy', 'gx'), may hold values 0 or 1
- obs_cell: int32 [2, 1024], replicated, may hold values from 0 to 262143, as said below
- obs_value: float32 [2, 1024], replicated, may hold values from 0.2 to 2
- observation_variance: float32 [2, 1024], replicated, may hold values from 0.05 to 0.5
- obs_perturb: float32 [2, 1024, 40], replicated, may hold values from -4 to 4
- radius: int32 [1], replicated, may hold values from 32 to 64
Outputs:
- analysis: float32 [40, 8, 64, 4096], P(None, None, 'gy', 'gx')
Inputs may be any that keep to these rules, and one draw needn't show every extreme that they name: obs_cell[b, k] is row * 4096 + column of the observed cell; with tiles of 4 rows and 128 columns, in each batch no tile holds more than 8 observed cells and some tile holds exactly 8.
All inputs are finite; a program needn't handle non-finite values. No bound on the sum of `land_sea` on one device may be relied on, other than what follows from the above.
Results may differ from a plain program's by a relative error of at most 0.0003.
Values sent between devices are 32-bit elements; how exact they have to be, the bound alone decides.
A program may use at most 64 MiB of HBM per device.

v0:
```python
import jax
import jax.numpy as jnp
from jax import lax
from jax.sharding import PartitionSpec as P

CAP = 8


def padded_2(x, sides, width):
    for axis, dim in sides:
        size, length = (lax.axis_size(axis), x.shape[dim])
        up = [(i, (i + 1) % size) for i in range(size)]
        down = [(j, i) for i, j in up]
        last = lax.slice_in_dim(x, length - width, length, axis=dim)
        initial = lax.slice_in_dim(x, 0, width, axis=dim)
        before = lax.ppermute(last, axis, up)
        after = lax.ppermute(initial, axis, down)
        x = jnp.concatenate([before, x, after], axis=dim)
    return x


def upwind(minus_two, minus_one, center, plus_one, plus_two, courant):
    rising = (2.0 * plus_one + 3.0 * center - 6.0 * minus_one + minus_two) / 6.0
    falling = (-plus_two + 6.0 * plus_one - 3.0 * center - 2.0 * minus_one) / 6.0
    return -(jnp.maximum(courant, 0.0) * rising + jnp.minimum(courant, 0.0) * falling)


def transport(padded, courant_x, courant_y, diffusion):
    row_count = padded.shape[-2] - 4
    columns = padded.shape[-1] - 4

    def offset(row_shift, col_shift):
        return padded[
            ..., 2 + row_shift : 2 + row_shift + row_count, 2 + col_shift : 2 + col_shift + columns
        ]

    center = offset(0, 0)
    along_x = upwind(
        offset(0, -2), offset(0, -1), center, offset(0, 1), offset(0, 2), courant_x[:, None]
    )
    along_y = upwind(
        offset(-2, 0), offset(-1, 0), center, offset(1, 0), offset(2, 0), courant_y[:, None]
    )
    spread = offset(0, 1) + offset(0, -1) + offset(1, 0) + offset(-1, 0) - 4.0 * center
    return (center, along_x + along_y + diffusion * spread)


def tendency(fields, growth, mixing):
    nutrient = fields[..., 0, :, :]
    plankton = fields[..., 1, :, :]
    grazer = fields[..., 2, :, :]
    detritus = fields[..., 3, :, :]
    uptake = growth * jnp.abs(nutrient) / (jnp.abs(nutrient) + 0.5) * plankton
    grazing = 0.3 * grazer * jnp.abs(plankton) / (jnp.abs(plankton) + 0.5)
    biology = jnp.stack(
        [
            -uptake + 0.1 * detritus,
            uptake - grazing - 0.05 * plankton,
            0.3 * grazing - 0.05 * grazer,
            0.7 * grazing + 0.05 * plankton + 0.05 * grazer - 0.1 * detritus,
        ],
        axis=-3,
    )
    upper_level = fields[..., 0, :, :, :]
    lower_level = fields[..., 1, :, :, :]
    vertical = jnp.stack(
        [mixing * (lower_level - upper_level), mixing * (upper_level - lower_level)], axis=-4
    )
    return biology + vertical


def build_slots(
    present_state,
    cells,
    values,
    variances,
    perturbs,
    tile_id,
    tiles_y,
    row_start,
    col_start,
    total_cols,
):
    members = present_state.shape[0]
    tile_rows = present_state.shape[2]
    tile_cols = present_state.shape[3]
    obs_rows = cells // total_cols
    obs_cols = cells % total_cols
    owners = obs_cols // tile_cols * tiles_y + obs_rows // tile_rows
    ownership_mask = owners == tile_id
    slot_rank = jnp.cumsum(ownership_mask.astype(jnp.int32)) - 1
    slot_hot = (slot_rank[None, :] == jnp.arange(CAP, dtype=jnp.int32)[:, None]) & ownership_mask[
        None, :
    ]
    slot_float = slot_hot.astype(jnp.float32)
    local_cell = (obs_rows - row_start) * tile_cols + (obs_cols - col_start)
    slot_cell = jnp.sum(jnp.where(slot_hot, local_cell[None, :], 0), axis=1)
    filled = jnp.sum(slot_float, axis=1)
    cell_hot = (
        (slot_cell[:, None] == jnp.arange(tile_rows * tile_cols, dtype=jnp.int32)[None, :])
        & (filled[:, None] > 0.0)
    ).astype(jnp.float32)
    plankton_field = present_state[:, 1].reshape(members, tile_rows * tile_cols)
    prior_slots = lax.dot_general(
        cell_hot, plankton_field, (((1,), (1,)), ((), ())), precision=lax.Precision.HIGHEST
    )
    slot_value = jnp.dot(slot_float, values, precision=lax.Precision.HIGHEST)
    slot_var = jnp.dot(slot_float, variances, precision=lax.Precision.HIGHEST)
    slot_noise = jnp.dot(slot_float, perturbs, precision=lax.Precision.HIGHEST)
    slot_row = jnp.dot(slot_float, obs_rows.astype(jnp.float32), precision=lax.Precision.HIGHEST)
    slot_col = jnp.dot(slot_float, obs_cols.astype(jnp.float32), precision=lax.Precision.HIGHEST)
    anomaly = prior_slots - jnp.mean(prior_slots, axis=1, keepdims=True)
    spread_var = jnp.sum(anomaly * anomaly, axis=1) / (members - 1)
    obs_scale = filled / ((members - 1) * (spread_var + slot_var + (1.0 - filled)))
    innovation = slot_value[:, None] + jnp.sqrt(slot_var)[:, None] * slot_noise - prior_slots
    record = jnp.concatenate(
        [anomaly, innovation, obs_scale[:, None], slot_row[:, None], slot_col[:, None]], axis=1
    )
    return record[None]


def local(
    ensemble,
    courant_x,
    courant_y,
    diffusion,
    mixing,
    growth,
    land_sea,
    obs_cell,
    obs_value,
    observation_variance,
    obs_perturb,
    radius,
):
    members, fields, tile_rows, tile_cols = ensemble.shape
    levels = courant_x.shape[0]
    tiles_x = lax.axis_size("gx")
    tiles_y = lax.axis_size("gy")
    tile_x = lax.axis_index("gx")
    tile_y = lax.axis_index("gy")
    total_cols = tile_cols * tiles_x
    total_rows = tile_rows * tiles_y
    ocean_mask = land_sea.astype(jnp.float32)
    padded = padded_2(ensemble, (("gx", 3), ("gy", 2)), 2)
    global_row = tile_y * tile_rows + jnp.arange(tile_rows + 4, dtype=jnp.int32) - 2
    inside = (global_row >= 0) & (global_row < total_rows)
    padded = jnp.where(inside[:, None], padded, 0.0)
    padded = padded.reshape(members, levels, fields // levels, tile_rows + 4, tile_cols + 4)
    center, carried = transport(padded, courant_x, courant_y, diffusion)
    present_state = center + ocean_mask * (carried + tendency(center, growth, mixing))
    present_state = present_state.reshape(members, fields, tile_rows, tile_cols)
    tile_id = tile_x * tiles_y + tile_y
    row_start = tile_y * tile_rows
    col_start = tile_x * tile_cols
    grid_cell_count = tile_rows * tile_cols
    cell_rowf = (
        jnp.broadcast_to(
            (row_start + jnp.arange(tile_rows, dtype=jnp.int32))[:, None], (tile_rows, tile_cols)
        )
        .reshape(grid_cell_count)
        .astype(jnp.float32)
    )
    cell_colf = (
        jnp.broadcast_to(
            (col_start + jnp.arange(tile_cols, dtype=jnp.int32))[None, :], (tile_rows, tile_cols)
        )
        .reshape(grid_cell_count)
        .astype(jnp.float32)
    )
    radius_sq = radius[0].astype(jnp.float32) * radius[0].astype(jnp.float32)
    half_cols = total_cols // 2
    for batch_index in range(obs_value.shape[0]):
        record = build_slots(
            present_state,
            obs_cell[batch_index],
            obs_value[batch_index],
            observation_variance[batch_index],
            obs_perturb[batch_index],
            tile_id,
            tiles_y,
            row_start,
            col_start,
            total_cols,
        )
        column_slots = lax.all_gather(record, "gy", axis=1, tiled=True)
        nearby = padded_2(column_slots, (("gx", 0),), 1)
        member_deviation = (present_state - jnp.mean(present_state, axis=0, keepdims=True)).reshape(
            members, fields * grid_cell_count
        )
        increment = jnp.zeros((members, fields * grid_cell_count), jnp.float32)
        for column_index in range(3):
            slot_block = nearby[column_index]
            block_size = slot_block.shape[0]
            slot_anom = slot_block[:, :members]
            slot_innov = slot_block[:, members : 2 * members]
            obs_scale = slot_block[:, 2 * members]
            slot_row = slot_block[:, 2 * members + 1]
            slot_col = slot_block[:, 2 * members + 2]
            col_gap = (
                jnp.mod(slot_col[:, None] - cell_colf[None, :] + half_cols, total_cols) - half_cols
            )
            row_gap = slot_row[:, None] - cell_rowf[None, :]
            taper_weight = jnp.maximum(
                0.0, 1.0 - (row_gap * row_gap + col_gap * col_gap) / radius_sq
            )
            weight = taper_weight * obs_scale[:, None]
            covariance = lax.dot_general(
                slot_anom,
                member_deviation,
                (((1,), (0,)), ((), ())),
                precision=lax.Precision.HIGHEST,
            )
            gain_block = (
                covariance.reshape(block_size, fields, grid_cell_count) * weight[:, None, :]
            ).reshape(block_size, fields * grid_cell_count)
            increment = increment + lax.dot_general(
                slot_innov, gain_block, (((0,), (0,)), ((), ())), precision=lax.Precision.HIGHEST
            )
        present_state = present_state + ocean_mask * increment.reshape(
            members, fields, tile_rows, tile_cols
        )
    return present_state


def solution(mesh):
    placed = (
        P(None, None, "gy", "gx"),
        P(None, "gy", "gx"),
        P(None, "gy", "gx"),
        P("gy", "gx"),
        P("gy", "gx"),
        P(None, "gy", "gx"),
        P("gy", "gx"),
        P(),
        P(),
        P(),
        P(),
        P(),
    )
    return jax.shard_map(
        local, mesh=mesh, in_specs=placed, out_specs=P(None, None, "gy", "gx"), check_vma=False
    )
```

profile of v0, /device:TPU:1, one launch (start us, length us, event | category | flops | bytes accessed | tf_op | source)
XLA Modules:
  0.0 205.8 jit_solution(6187460439538034503)
XLA Ops:
  0.0 1.8 fusion.195
  1.8 0.4 copy.201
  2.2 14.5 %collective-permute-start.1 = (f32[40,8,4,2]{0,1,3,2:T(8,128)S(1)}, f32[40,8,4,2]{0,1,3,2:T(8,128)S(1)}, u32[]{:S(2)}, u32[]{:S(2)}) collective-permute-start(f32[40,8,4,2]{0,1,3,2:T(8,128)S(1)} %copy.201), channel_id=1, source_target_pairs={{16,0},{32,16},{48,32},{64,48},{80,64},{96,80},{112,96},{128,112},... | collective-permute-start | bytes 30728 | tf_op jit(solution)/shard_map/ppermute | solution.py:17
  16.8 0.4 copy.200
  17.2 1.9 collective-permute-start
  19.4 0.3 reduce-window.16
  20.5 0.3 reduce-window.24
  21.3 0.6 select_reduce_fusion
  21.9 0.5 broadcast_compare_fusion
  22.4 0.7 convolution_bitcast_fusion.5
  23.2 0.7 convolution_bitcast_fusion.1
  23.9 0.7 convolution_bitcast_fusion
  25.5 0.6 copy.156
  26.2 0.6 copy.154
  26.8 0.6 pad_maximum_fusion
  27.5 3.6 %collective-permute-start.3 = (f32[40,8,2,132]{3,1,2,0:T(8,128)S(1)}, f32[40,8,2,132]{3,1,2,0:T(8,128)S(1)}, u32[]{:S(2)}, u32[]{:S(2)}) collective-permute-start(f32[40,8,2,132]{3,1,2,0:T(8,128)S(1)} %get-tuple-element.42), channel_id=1, source_target_pairs={{1,0},{2,1},{3,2},{4,3},{5,4},{6,5},{7,6},{8,7},{9,8},{10,9},{11,1... | collective-permute-start | bytes 1013768 | tf_op jit(solution)/shard_map/ppermute | solution.py:17
  31.1 5.8 %collective-permute-start.2 = (f32[40,8,2,132]{3,1,2,0:T(8,128)S(1)}, f32[40,8,2,132]{3,1,2,0:T(8,128)S(1)}, u32[]{:S(2)}, u32[]{:S(2)}) collective-permute-start(f32[40,8,2,132]{3,1,2,0:T(8,128)S(1)} %get-tuple-element.41), channel_id=1, source_target_pairs={{0,1},{1,2},{2,3},{3,4},{4,5},{5,6},{6,7},{7,8},{8,9},{9,10},{10,1... | collective-permute-start | bytes 1013768 | tf_op jit(solution)/shard_map/ppermute | solution.py:16
  37.2 0.8 copy.158
  37.9 21.4 %collective-permute-done.3 = f32[40,8,2,132]{3,1,2,0:T(8,128)S(1)} collective-permute-done((f32[40,8,2,132]{3,1,2,0:T(8,128)S(1)}, f32[40,8,2,132]{3,1,2,0:T(8,128)S(1)}, u32[]{:S(2)}, u32[]{:S(2)}) %collective-permute-start.3) | collective-permute-done | bytes 337952 | tf_op jit(solution)/shard_map/ppermute | solution.py:17
  59.4 0.4 copy.159
  59.8 0.4 copy.157
  60.2 0.3 maximum_select_fusion
  60.5 0.3 copy-done.19
  60.8 0.2 subtract_multiply_fusion.1
  61.1 0.2 negate_add_fusion
  61.5 1.5 fusion.192
  63.1 0.3 fusion.197
  64.1 27.1 %all-gather = f32[128,83]{1,0:T(8,128)S(1)} all-gather(f32[8,83]{1,0:T(8,128)S(1)} %concatenate.24), channel_id=2, replica_groups=mesh['gx'=32,'gy'=16] {'gy'}, dimensions={0}, use_global_device_ids=true | all-gather | bytes 45152 | tf_op jit(solution)/shard_map/all_gather | solution.py:186
  91.2 5.3 %collective-permute-start.4 = (f32[1,128,83]{2,1,0:T(8,128)S(1)}, f32[1,128,83]{2,1,0:T(8,128)S(1)}, u32[]{:S(2)}, u32[]{:S(2)}) collective-permute-start(f32[1,128,83]{2,1,0:T(8,128)S(1)} %bitcast.182), channel_id=1, source_target_pairs={{0,16},{16,32},{32,48},{48,64},{64,80},{80,96},{96,112},{112,128},... | collective-permute-start | bytes 127496 | tf_op jit(solution)/shard_map/ppermute | solution.py:16
  96.6 7.9 %collective-permute-start.5 = (f32[1,128,83]{2,1,0:T(8,128)S(1)}, f32[1,128,83]{2,1,0:T(8,128)S(1)}, u32[]{:S(2)}, u32[]{:S(2)}) collective-permute-start(f32[1,128,83]{2,1,0:T(8,128)S(1)} %bitcast.183), channel_id=1, source_target_pairs={{16,0},{32,16},{48,32},{64,48},{80,64},{96,80},{112,96},{128,112},... | collective-permute-start | bytes 127496 | tf_op jit(solution)/shard_map/ppermute | solution.py:17
  104.6 0.3 reshape.696
  105.2 0.2 slice_reduce_fusion.17
  105.8 1.5 fusion.95
  107.3 3.1 %convolution_multiply_fusion.3 = f32[128,8,512]{2,0,1:T(8,128)} fusion(f32[128,512]{1,0:T(8,128)S(1)} %get-tuple-element.57, f32[5,8,8,512]{3,2,1,0:T(8,128)S(1)} %bitcast.166, f32[128,83]{1,0:T(8,128)S(1)} %bitcast.194), kind=kOutput, calls=%fused_computation.8 | convolution fusion | flops 252182528 | bytes 3057152 | tf_op jit(solution)/shard_map/dot_general | solution.py:208
  110.5 1.9 copy.173
  112.4 4.0 %fusion.117 = f32[40,4096]{1,0:T(8,128)} fusion(f32[128,4096]{0,1:T(8,128)S(1)} %bitcast.171, f32[128,83]{1,0:T(8,128)} %bitcast.195), kind=kOutput, calls=%fused_computation.187 | convolution fusion | flops 251658240 | bytes 2795008 | tf_op jit(solution)/shard_map/dot_general | solution.py:217
  116.4 3.1 %convolution_multiply_fusion.4 = f32[128,8,512]{2,0,1:T(8,128)} fusion(f32[128,512]{1,0:T(8,128)S(1)} %copy-done.8, f32[5,8,8,512]{3,2,1,0:T(8,128)S(1)} %bitcast.167, f32[128,83]{1,0:T(8,128)S(1)} %all-gather), kind=kOutput, calls=%fused_computation.9 | convolution fusion | flops 252182528 | bytes 3057152 | tf_op jit(solution)/shard_map/dot_general | solution.py:208
  119.6 1.9 copy.170
  121.5 3.2 %fusion.119 = f32[40,4096]{1,0:T(8,128)} fusion(f32[128,4096]{0,1:T(8,128)S(1)} %bitcast.172, f32[128,83]{1,0:T(8,128)S(1)} %all-gather), kind=kOutput, calls=%fused_computation.193 | convolution fusion | flops 251658240 | bytes 2795008 | tf_op jit(solution)/shard_map/dot_general | solution.py:217
  124.7 3.1 %convolution_multiply_fusion.5 = f32[128,8,512]{2,0,1:T(8,128)} fusion(f32[128,512]{1,0:T(8,128)S(1)} %copy-done.6, f32[5,8,8,512]{3,2,1,0:T(8,128)S(1)} %bitcast.168, f32[128,83]{1,0:T(8,128)S(1)} %bitcast.188), kind=kOutput, calls=%fused_computation.10 | convolution fusion | flops 252182528 | bytes 3057152 | tf_op jit(solution)/shard_map/dot_general | solution.py:208
  127.8 1.9 copy.167
  129.7 3.6 %fusion.1 = f32[40,4096]{1,0:T(8,128)S(1)} fusion(f32[40,4096]{1,0:T(8,128)} %fusion.117, f32[40,4096]{1,0:T(8,128)} %fusion.119, f32[128,4096]{0,1:T(8,128)S(1)} %bitcast.169, f32[128,83]{1,0:T(8,128)S(1)} %bitcast.189), kind=kOutput, calls=%fused_computation.3 | convolution fusion | flops 251985920 | bytes 4105728 | tf_op jit(solution)/shard_map/dot_general | solution.py:217
  133.4 0.4 reshape.700
  133.9 0.2 copy_add_fusion
  134.2 0.3 fusion.198
  135.3 29.8 %all-gather.1 = f32[128,83]{1,0:T(8,128)S(1)} all-gather(f32[8,83]{1,0:T(8,128)S(1)} %concatenate.25), channel_id=3, replica_groups=mesh['gx'=32,'gy'=16] {'gy'}, dimensions={0}, use_global_device_ids=true | all-gather | bytes 45152 | tf_op jit(solution)/shard_map/all_gather | solution.py:186
  165.0 1.9 collective-permute-start.6
  167.0 8.2 %collective-permute-start.7 = (f32[1,128,83]{2,1,0:T(8,128)S(1)}, f32[1,128,83]{2,1,0:T(8,128)S(1)}, u32[]{:S(2)}, u32[]{:S(2)}) collective-permute-start(f32[1,128,83]{2,1,0:T(8,128)S(1)} %bitcast.181), channel_id=1, source_target_pairs={{16,0},{32,16},{48,32},{64,48},{80,64},{96,80},{112,96},{128,112},... | collective-permute-start | bytes 127496 | tf_op jit(solution)/shard_map/ppermute | solution.py:17
  175.2 0.4 reshape.702
  175.6 0.4 fusion.35
  176.4 0.2 slice_reduce_fusion.8
  176.6 0.2 slice_reduce_fusion.2
  176.9 1.5 fusion.86
  178.4 3.1 %convolution_multiply_fusion = f32[128,8,512]{2,0,1:T(8,128)} fusion(f32[128,512]{1,0:T(8,128)S(1)} %get-tuple-element.52, f32[5,8,8,512]{3,2,1,0:T(8,128)S(1)} %bitcast.163, f32[128,83]{1,0:T(8,128)S(1)} %bitcast.191), kind=kOutput, calls=%fused_computation.5 | convolution fusion | flops 252182528 | bytes 3057152 | tf_op jit(solution)/shard_map/dot_general | solution.py:208
  181.5 1.9 copy.187
  183.4 4.0 %fusion.112 = f32[40,4096]{1,0:T(8,128)} fusion(f32[128,4096]{0,1:T(8,128)S(1)} %bitcast.173, f32[128,83]{1,0:T(8,128)} %bitcast.192), kind=kOutput, calls=%fused_computation.170 | convolution fusion | flops 251658240 | bytes 2795008 | tf_op jit(solution)/shard_map/dot_general | solution.py:217
  187.5 3.1 %convolution_multiply_fusion.1 = f32[128,8,512]{2,0,1:T(8,128)} fusion(f32[128,512]{1,0:T(8,128)S(1)} %copy-done.7, f32[5,8,8,512]{3,2,1,0:T(8,128)S(1)} %bitcast.164, f32[128,83]{1,0:T(8,128)S(1)} %all-gather.1), kind=kOutput, calls=%fused_computation.6 | convolution fusion | flops 252182528 | bytes 3057152 | tf_op jit(solution)/shard_map/dot_general | solution.py:208
  190.6 1.9 copy.184
  192.5 3.2 %fusion.114 = f32[40,4096]{1,0:T(8,128)} fusion(f32[128,4096]{0,1:T(8,128)S(1)} %bitcast.174, f32[128,83]{1,0:T(8,128)S(1)} %all-gather.1), kind=kOutput, calls=%fused_computation.176 | convolution fusion | flops 251658240 | bytes 2795008 | tf_op jit(solution)/shard_map/dot_general | solution.py:217
  195.7 3.1 %convolution_multiply_fusion.2 = f32[128,8,512]{2,0,1:T(8,128)} fusion(f32[128,512]{1,0:T(8,128)S(1)} %copy-done.5, f32[5,8,8,512]{3,2,1,0:T(8,128)S(1)} %bitcast.165, f32[128,83]{1,0:T(8,128)S(1)} %bitcast.185), kind=kOutput, calls=%fused_computation.7 | convolution fusion | flops 252182528 | bytes 3057152 | tf_op jit(solution)/shard_map/dot_general | solution.py:208
  198.8 1.9 copy.181
  200.7 3.6 %fusion = f32[40,4096]{1,0:T(8,128)S(1)} fusion(f32[40,4096]{1,0:T(8,128)} %fusion.112, f32[40,4096]{1,0:T(8,128)} %fusion.114, f32[128,4096]{0,1:T(8,128)S(1)} %bitcast.170, f32[128,83]{1,0:T(8,128)S(1)} %bitcast.186), kind=kOutput, calls=%fused_computation.1 | convolution fusion | flops 251985920 | bytes 4105728 | tf_op jit(solution)/shard_map/dot_general | solution.py:217
  204.3 0.4 reshape.706
  204.8 1.0 multiply_add_fusion.2
  (121 shorter events, 4.8 us)
Async XLA Ops:
  0.0 24.8 %copy-start = (f32[40,8,4,128]{3,2,1,0:T(4,128)S(1)}, f32[40,8,4,128]{3,2,1,0:T(4,128)}, u32[]{:S(2)}) copy-start(f32[40,8,4,128]{3,2,1,0:T(4,128)} %param.12) | copy-start | bytes 1966084
  0.0 19.1 %copy-start.11 = (s32[2,1024]{1,0:T(2,128)S(1)}, s32[2,1024]{1,0:T(2,128)}, u32[]{:S(2)}) copy-start(s32[2,1024]{1,0:T(2,128)} %param.19) | copy-start | bytes 24580
  0.0 22.4 %copy-start.26 = (f32[2,1024]{1,0:T(2,128)S(1)}, f32[2,1024]{1,0:T(2,128)}, u32[]{:S(2)}) copy-start(f32[2,1024]{1,0:T(2,128)} %param.20) | copy-start | bytes 24580
  1.8 23.0 %copy-start.21 = (s32[4,128]{1,0:T(4,128)S(1)}, s32[4,128]{1,0:T(4,128)}, u32[]{:S(2)}) copy-start(s32[4,128]{1,0:T(4,128)} %param.18) | copy-start | bytes 6148
  2.2 23.3 %collective-permute-start.1 = (f32[40,8,4,2]{0,1,3,2:T(8,128)S(1)}, f32[40,8,4,2]{0,1,3,2:T(8,128)S(1)}, u32[]{:S(2)}, u32[]{:S(2)}) collective-permute-start(f32[40,8,4,2]{0,1,3,2:T(8,128)S(1)} %copy.201), channel_id=1, source_target_pairs={{16,0},{32,16},{48,32},{64,48},{80,64},{96,80},{112,96},{128,112},... | collective-permute-start | bytes 30728 | tf_op jit(solution)/shard_map/ppermute | solution.py:17
  17.2 8.9 %collective-permute-start = (f32[40,8,4,2]{0,1,3,2:T(8,128)S(1)}, f32[40,8,4,2]{0,1,3,2:T(8,128)S(1)}, u32[]{:S(2)}, u32[]{:S(2)}) collective-permute-start(f32[40,8,4,2]{0,1,3,2:T(8,128)S(1)} %copy.200), channel_id=1, source_target_pairs={{0,16},{16,32},{32,48},{48,64},{64,80},{80,96},{96,112},{112,128},... | collective-permute-start | bytes 30728 | tf_op jit(solution)/shard_map/ppermute | solution.py:16
  19.3 6.8 %copy-start.12 = (pred[1024]{0:T(1024)(128)(4,1)}, pred[1024]{0:T(1024)(128)(4,1)S(1)}, u32[]{:S(2)}) copy-start(pred[1024]{0:T(1024)(128)(4,1)S(1)} %get-tuple-element.25) | copy-start | bytes 3076
  21.3 1.9 copy-start.24
  27.4 9.7 %copy-start.15 = (f32[2,4,128]{2,1,0:T(4,128)S(1)}, f32[2,4,128]{2,1,0:T(4,128)}, u32[]{:S(2)}) copy-start(f32[2,4,128]{2,1,0:T(4,128)} %param.14) | copy-start | bytes 12292
  27.4 9.7 %copy-start.16 = (f32[2,4,128]{2,1,0:T(4,128)S(1)}, f32[2,4,128]{2,1,0:T(4,128)}, u32[]{:S(2)}) copy-start(f32[2,4,128]{2,1,0:T(4,128)} %param.13) | copy-start | bytes 12292
  27.5 31.9 %collective-permute-start.3 = (f32[40,8,2,132]{3,1,2,0:T(8,128)S(1)}, f32[40,8,2,132]{3,1,2,0:T(8,128)S(1)}, u32[]{:S(2)}, u32[]{:S(2)}) collective-permute-start(f32[40,8,2,132]{3,1,2,0:T(8,128)S(1)} %get-tuple-element.42), channel_id=1, source_target_pairs={{1,0},{2,1},{3,2},{4,3},{5,4},{6,5},{7,6},{8,7},{9,8},{10,9},{11,1... | collective-permute-start | bytes 1013768 | tf_op jit(solution)/shard_map/ppermute | solution.py:17
  31.1 28.6 %collective-permute-start.2 = (f32[40,8,2,132]{3,1,2,0:T(8,128)S(1)}, f32[40,8,2,132]{3,1,2,0:T(8,128)S(1)}, u32[]{:S(2)}, u32[]{:S(2)}) collective-permute-start(f32[40,8,2,132]{3,1,2,0:T(8,128)S(1)} %get-tuple-element.41), channel_id=1, source_target_pairs={{0,1},{1,2},{2,3},{3,4},{4,5},{5,6},{6,7},{7,8},{8,9},{9,10},{10,1... | collective-permute-start | bytes 1013768 | tf_op jit(solution)/shard_map/ppermute | solution.py:16
  60.2 0.7 copy-start.19
  60.2 0.9 copy-start.14
  60.8 0.7 copy-start.20
  61.5 2.0 copy-start.27
  61.5 2.3 %copy-start.9 = (f32[2,1024,40]{1,2,0:T(8,128)S(1)}, f32[2,1024,40]{1,2,0:T(8,128)}, u32[]{:S(2)}) copy-start(f32[2,1024,40]{1,2,0:T(8,128)} %param.22) | copy-start | bytes 983044
  91.2 14.0 %collective-permute-start.4 = (f32[1,128,83]{2,1,0:T(8,128)S(1)}, f32[1,128,83]{2,1,0:T(8,128)S(1)}, u32[]{:S(2)}, u32[]{:S(2)}) collective-permute-start(f32[1,128,83]{2,1,0:T(8,128)S(1)} %bitcast.182), channel_id=1, source_target_pairs={{0,16},{16,32},{32,48},{48,64},{64,80},{80,96},{96,112},{112,128},... | collective-permute-start | bytes 127496 | tf_op jit(solution)/shard_map/ppermute | solution.py:16
  96.6 9.0 %collective-permute-start.5 = (f32[1,128,83]{2,1,0:T(8,128)S(1)}, f32[1,128,83]{2,1,0:T(8,128)S(1)}, u32[]{:S(2)}, u32[]{:S(2)}) collective-permute-start(f32[1,128,83]{2,1,0:T(8,128)S(1)} %bitcast.183), channel_id=1, source_target_pairs={{16,0},{32,16},{48,32},{64,48},{80,64},{96,80},{112,96},{128,112},... | collective-permute-start | bytes 127496 | tf_op jit(solution)/shard_map/ppermute | solution.py:17
  104.9 2.4 %copy-start.1 = (f32[40,4096]{1,0:T(8,128)}, f32[40,4096]{1,0:T(8,128)S(1)}, u32[]{:S(2)}) copy-start(f32[40,4096]{1,0:T(8,128)S(1)} %reshape.696) | copy-start | bytes 1966084
  105.6 1.8 copy-start.4
  112.4 4.0 %copy-start.8 = (f32[128,512]{1,0:T(8,128)S(1)}, f32[128,512]{1,0:T(8,128)}, u32[]{:S(2)}) copy-start(f32[128,512]{1,0:T(8,128)} %get-tuple-element.56) | copy-start | bytes 786436
  121.5 3.2 %copy-start.6 = (f32[128,512]{1,0:T(8,128)S(1)}, f32[128,512]{1,0:T(8,128)}, u32[]{:S(2)}) copy-start(f32[128,512]{1,0:T(8,128)} %get-tuple-element.55) | copy-start | bytes 786436
  133.3 0.8 copy-start.23
  133.3 0.8 copy-start.29
  133.3 1.3 copy-start.13
  133.3 1.3 copy-start.25
  133.4 1.3 copy-start.28
  133.4 1.6 copy-start.10
  133.4 1.6 copy-start.22
  133.4 1.7 copy-start.17
  133.4 1.8 copy-start.18
  134.1 42.0 %copy-start.2 = (f32[40,4096]{1,0:T(8,128)S(1)}, f32[40,4096]{1,0:T(8,128)}, u32[]{:S(2)}) copy-start(f32[40,4096]{1,0:T(8,128)} %copy-done.1) | copy-start | bytes 1966084
  165.0 11.3 %collective-permute-start.6 = (f32[1,128,83]{2,1,0:T(8,128)S(1)}, f32[1,128,83]{2,1,0:T(8,128)S(1)}, u32[]{:S(2)}, u32[]{:S(2)}) collective-permute-start(f32[1,128,83]{2,1,0:T(8,128)S(1)} %bitcast.180), channel_id=1, source_target_pairs={{0,16},{16,32},{32,48},{48,64},{64,80},{80,96},{96,112},{112,128},... | collective-permute-start | bytes 127496 | tf_op jit(solution)/shard_map/ppermute | solution.py:16
  167.0 9.7 %collective-permute-start.7 = (f32[1,128,83]{2,1,0:T(8,128)S(1)}, f32[1,128,83]{2,1,0:T(8,128)S(1)}, u32[]{:S(2)}, u32[]{:S(2)}) collective-permute-start(f32[1,128,83]{2,1,0:T(8,128)S(1)} %bitcast.181), channel_id=1, source_target_pairs={{16,0},{32,16},{48,32},{64,48},{80,64},{96,80},{112,96},{128,112},... | collective-permute-start | bytes 127496 | tf_op jit(solution)/shard_map/ppermute | solution.py:17
  176.6 1.8 copy-start.3
  183.4 4.0 %copy-start.7 = (f32[128,512]{1,0:T(8,128)S(1)}, f32[128,512]{1,0:T(8,128)}, u32[]{:S(2)}) copy-start(f32[128,512]{1,0:T(8,128)} %get-tuple-element.51) | copy-start | bytes 786436
  192.5 3.2 %copy-start.5 = (f32[128,512]{1,0:T(8,128)S(1)}, f32[128,512]{1,0:T(8,128)}, u32[]{:S(2)}) copy-start(f32[128,512]{1,0:T(8,128)} %get-tuple-element.50) | copy-start | bytes 786436
where the time goes:
time: 206 us
  blocking collectives  56.9 us (28%)
  starting transfers between devices  49.2 us (24%)
  matrix products  44.2 us (21%)
  local copies, waits for them, and re-layouts  21.7 us (11%)
  waiting for transfers between devices  21.6 us (10%)
  other arithmetic  10.6 us (5%)
    all_gather x2, blocking collectives, local(): column_slots = lax.all_gather(record, 'gy', axis=1, tiled=True)  56.9 us
    ppermute x4, starting transfers between devices, padded_2(): after = lax.ppermute(initial, axis, down)  34.2 us
    dot_general x6, matrix products, local(): lax.dot_general(slot_innov, gain_block, (((0,), (0,)), ((), ())), precisi...  21.6 us
    ppermute x4, waiting for transfers between devices, padded_2(): after = lax.ppermute(initial, axis, down)  21.6 us
    dot_general x6, matrix products, local(): lax.dot_general(slot_anom, member_deviation, (((1,), (0,)), ((), ())), pr...  18.8 us
    ppermute x4, starting transfers between devices, padded_2(): before = lax.ppermute(last, axis, up)  15 us
    mul x6, local copies, waits for them, and re-layouts, local(): covariance.reshape(block_size, fields, grid_cell_count) * weight[:, None, :]  11.4 us
  transfers between devices with their start and end apart: 8, of which 2 were waited for; matrix products, arithmetic and copies ran while one was open for 5% of the time, Pallas kernels for 0%

commit v1 on v0

--- a/solution.py
+++ b/solution.py
@@ -183,7 +183,9 @@
             col_start,
             total_cols,
         )
-        column_slots = lax.all_gather(record, "gy", axis=1, tiled=True)
+        column_slots = jnp.concatenate(
+            lax.all_to_all(jnp.stack([record] * lax.axis_size("gy")), "gy", 0, 0), axis=1
+        )
         nearby = padded_2(column_slots, (("gx", 0),), 1)
         member_deviation = (present_state - jnp.mean(present_state, axis=0, keepdims=True)).reshape(
             members, fields * grid_cell_count

time: 206 us -> 181 us (0.88)
  blocking collectives: 56.9 us -> 0 us
  waiting for transfers between devices: 21.6 us -> 41.6 us
  starting transfers between devices: 49.2 us -> 59.7 us
    all_gather x2 -> x0, blocking collectives: 56.9 us -> none  [local(): column_slots = lax.all_gather(record, 'gy', axis=1, tiled=True)]
    all_to_all x0 -> x2, waiting for transfers between devices: none -> 18.6 us  [local(): lax.all_to_all(jnp.stack([record] * lax.axis_size('gy')), 'gy', 0, 0)]
    all_to_all x0 -> x2, starting transfers between devices: none -> 10.2 us  [local(): lax.all_to_all(jnp.stack([record] * lax.axis_size('gy')), 'gy', 0, 0)]
  transfers between devices with their start and end apart: 8 -> 10, of which waited for: 2 -> 6; matrix products, arithmetic and copies ran while one was open for 5% -> 4% of each run, Pallas kernels for 0% -> 0%
where the time goes in v1:
time: 181 us; the launch traced here: 180 us
  starting transfers between devices  59.7 us (33%)
  matrix products  43.2 us (24%)
  waiting for transfers between devices  41.6 us (23%)
  local copies, waits for them, and re-layouts  23.1 us (13%)
  other arithmetic  11.4 us (6%)
    ppermute x4, starting transfers between devices, padded_2(): after = lax.ppermute(initial, axis, down)  33.9 us
    dot_general x6, matrix products, local(): lax.dot_general(slot_innov, gain_block, (((0,), (0,)), ((), ())), precisi...  21.2 us
    ppermute x4, waiting for transfers between devices, padded_2(): after = lax.ppermute(initial, axis, down)  21.2 us
    dot_general x6, matrix products, local(): lax.dot_general(slot_anom, member_deviation, (((1,), (0,)), ((), ())), pr...  19 us
    all_to_all x2, waiting for transfers between devices, local(): lax.all_to_all(jnp.stack([record] * lax.axis_size('gy')), 'gy', 0, 0)  18.6 us
    ppermute x4, starting transfers between devices, padded_2(): before = lax.ppermute(last, axis, up)  15.7 us
    mul x6, local copies, waits for them, and re-layouts, local(): covariance.reshape(block_size, fields, grid_cell_count) * weight[:, None, :]  11.4 us
    all_to_all x2, starting transfers between devices, local(): lax.all_to_all(jnp.stack([record] * lax.axis_size('gy')), 'gy', 0, 0)  10.2 us
  transfers between devices with their start and end apart: 10, of which 6 were waited for; matrix products, arithmetic and copies ran while one was open for 4% of the time, Pallas kernels for 0%

profile of v1, /device:TPU:1, one launch (start us, length us, event | category | flops | bytes accessed | tf_op | source)
XLA Modules:
  0.0 180.4 jit_solution(12430591568962906472)
XLA Ops:
  0.0 1.8 fusion.195
  1.8 0.4 copy.209
  2.2 14.5 %collective-permute-start.1 = (f32[40,8,4,2]{0,1,3,2:T(8,128)S(1)}, f32[40,8,4,2]{0,1,3,2:T(8,128)S(1)}, u32[]{:S(2)}, u32[]{:S(2)}) collective-permute-start(f32[40,8,4,2]{0,1,3,2:T(8,128)S(1)} %copy.209), channel_id=1, source_target_pairs={{16,0},{32,16},{48,32},{64,48},{80,64},{96,80},{112,96},{128,112},... | collective-permute-start | bytes 30728 | tf_op jit(solution)/shard_map/ppermute | solution.py:17
  16.8 0.4 copy.208
  17.2 1.9 %collective-permute-start = (f32[40,8,4,2]{0,1,3,2:T(8,128)S(1)}, f32[40,8,4,2]{0,1,3,2:T(8,128)S(1)}, u32[]{:S(2)}, u32[]{:S(2)}) collective-permute-start(f32[40,8,4,2]{0,1,3,2:T(8,128)S(1)} %copy.208), channel_id=1, source_target_pairs={{0,16},{16,32},{32,48},{48,64},{64,80},{80,96},{96,112},{112,128},... | collective-permute-start | bytes 30728 | tf_op jit(solution)/shard_map/ppermute | solution.py:16
  19.4 0.3 reduce-window.16
  20.5 0.3 reduce-window.24
  21.4 0.6 broadcast_compare_fusion
  23.3 0.6 copy.176
  23.9 1.8 %collective-permute-done = f32[40,8,4,2]{0,1,3,2:T(8,128)S(1)} collective-permute-done((f32[40,8,4,2]{0,1,3,2:T(8,128)S(1)}, f32[40,8,4,2]{0,1,3,2:T(8,128)S(1)}, u32[]{:S(2)}, u32[]{:S(2)}) %collective-permute-start) | collective-permute-done | bytes 10272 | tf_op jit(solution)/shard_map/ppermute | solution.py:16
  25.8 0.6 copy.174
  26.4 0.6 pad_maximum_fusion
  27.1 4.0 %collective-permute-start.3 = (f32[40,8,2,132]{3,1,2,0:T(8,128)S(1)}, f32[40,8,2,132]{3,1,2,0:T(8,128)S(1)}, u32[]{:S(2)}, u32[]{:S(2)}) collective-permute-start(f32[40,8,2,132]{3,1,2,0:T(8,128)S(1)} %get-tuple-element.30), channel_id=1, source_target_pairs={{1,0},{2,1},{3,2},{4,3},{5,4},{6,5},{7,6},{8,7},{9,8},{10,9},{11,1... | collective-permute-start | bytes 1013768 | tf_op jit(solution)/shard_map/ppermute | solution.py:17
  31.1 5.5 %collective-permute-start.2 = (f32[40,8,2,132]{3,1,2,0:T(8,128)S(1)}, f32[40,8,2,132]{3,1,2,0:T(8,128)S(1)}, u32[]{:S(2)}, u32[]{:S(2)}) collective-permute-start(f32[40,8,2,132]{3,1,2,0:T(8,128)S(1)} %get-tuple-element.29), channel_id=1, source_target_pairs={{0,1},{1,2},{2,3},{3,4},{4,5},{5,6},{6,7},{7,8},{8,9},{9,10},{10,1... | collective-permute-start | bytes 1013768 | tf_op jit(solution)/shard_map/ppermute | solution.py:16
  36.8 0.8 copy.178
  37.5 19.6 %collective-permute-done.3 = f32[40,8,2,132]{3,1,2,0:T(8,128)S(1)} collective-permute-done((f32[40,8,2,132]{3,1,2,0:T(8,128)S(1)}, f32[40,8,2,132]{3,1,2,0:T(8,128)S(1)}, u32[]{:S(2)}, u32[]{:S(2)}) %collective-permute-start.3) | collective-permute-done | bytes 337952 | tf_op jit(solution)/shard_map/ppermute | solution.py:17
  57.2 0.4 copy.179
  57.6 0.4 copy.177
  58.0 0.3 maximum_select_fusion
  58.3 0.3 copy-done.14
  58.9 0.2 negate_add_fusion
  59.3 1.5 fusion.192
  61.1 0.3 fusion.197
  62.1 0.7 stack.20
  62.8 5.1 %all-to-all-start = ((f32[16,1,8,83]{3,2,1,0:T(8,128)}), f32[16,1,8,83]{3,2,1,0:T(8,128)S(1)}, u32[]{:S(2)}, u32[]{:S(2)}) async-start(f32[16,1,8,83]{3,2,1,0:T(8,128)} %stack.20), calls=%async_computation | async-start | bytes 131072 | tf_op jit(solution)/shard_map/all_to_all | solution.py:187
  67.9 0.3 reshape.707
  68.2 9.4 %all-to-all-done = f32[16,1,8,83]{3,2,1,0:T(8,128)S(1)} async-done(((f32[16,1,8,83]{3,2,1,0:T(8,128)}), f32[16,1,8,83]{3,2,1,0:T(8,128)S(1)}, u32[]{:S(2)}, u32[]{:S(2)}) %all-to-all-start) | async-done | bytes 42528 | tf_op jit(solution)/shard_map/all_to_all | solution.py:187
  77.7 6.4 %collective-permute-start.4 = (f32[1,128,83]{1,2,0:T(8,128)S(1)}, f32[1,128,83]{1,2,0:T(8,128)S(1)}, u32[]{:S(2)}, u32[]{:S(2)}) collective-permute-start(f32[1,128,83]{1,2,0:T(8,128)S(1)} %copy.184), channel_id=1, source_target_pairs={{0,16},{16,32},{32,48},{48,64},{64,80},{80,96},{96,112},{112,128},... | collective-permute-start | bytes 127496 | tf_op jit(solution)/shard_map/ppermute | solution.py:16
  84.1 7.2 %collective-permute-start.5 = (f32[1,128,83]{1,2,0:T(8,128)S(1)}, f32[1,128,83]{1,2,0:T(8,128)S(1)}, u32[]{:S(2)}, u32[]{:S(2)}) collective-permute-start(f32[1,128,83]{1,2,0:T(8,128)S(1)} %copy.184), channel_id=1, source_target_pairs={{16,0},{32,16},{48,32},{64,48},{80,64},{96,80},{112,96},{128,112},... | collective-permute-start | bytes 127496 | tf_op jit(solution)/shard_map/ppermute | solution.py:17
  91.6 0.9 collective-permute-done.5
  92.4 1.5 fusion.95
  94.0 3.2 %convolution_multiply_fusion.3 = f32[128,8,512]{2,0,1:T(8,128)} fusion(f32[128,512]{1,0:T(8,128)S(1)} %get-tuple-element.57, f32[5,8,8,512]{3,2,1,0:T(8,128)S(1)} %bitcast.194, f32[128,83]{0,1:T(8,128)S(1)} %bitcast.231), kind=kOutput, calls=%fused_computation.8 | convolution fusion | flops 252182528 | bytes 3035136 | tf_op jit(solution)/shard_map/dot_general | solution.py:210
  97.2 1.9 %copy.193 = f32[128,8,512]{0,2,1:T(8,128)S(1)} copy(f32[128,8,512]{2,0,1:T(8,128)} %convolution_multiply_fusion.3) | data formatting | bytes 4194304 | tf_op jit(solution)/shard_map/mul | solution.py:217
  99.1 3.9 %fusion.131 = f32[40,4096]{1,0:T(8,128)} fusion(f32[128,4096]{0,1:T(8,128)S(1)} %bitcast.199, f32[128,83]{0,1:T(8,128)} %bitcast.232), kind=kOutput, calls=%fused_computation.192 | convolution fusion | flops 251658240 | bytes 2772992 | tf_op jit(solution)/shard_map/dot_general | solution.py:219
  103.0 3.1 %convolution_multiply_fusion.4 = f32[128,8,512]{2,0,1:T(8,128)} fusion(f32[128,512]{1,0:T(8,128)S(1)} %copy-done.6, f32[5,8,8,512]{3,2,1,0:T(8,128)S(1)} %bitcast.195, f32[128,83]{1,0:T(8,128)S(1)} %bitcast.210), kind=kOutput, calls=%fused_computation.9 | convolution fusion | flops 252182528 | bytes 3057152 | tf_op jit(solution)/shard_map/dot_general | solution.py:210
  106.1 1.9 %copy.190 = f32[128,8,512]{0,2,1:T(8,128)S(1)} copy(f32[128,8,512]{2,0,1:T(8,128)} %convolution_multiply_fusion.4) | data formatting | bytes 4194304 | tf_op jit(solution)/shard_map/mul | solution.py:217
  108.0 3.2 %fusion.114 = f32[40,4096]{1,0:T(8,128)} fusion(f32[128,4096]{0,1:T(8,128)S(1)} %bitcast.200, f32[128,83]{1,0:T(8,128)S(1)} %bitcast.211), kind=kOutput, calls=%fused_computation.176 | convolution fusion | flops 251658240 | bytes 2795008 | tf_op jit(solution)/shard_map/dot_general | solution.py:219
  111.2 3.2 %convolution_multiply_fusion.5 = f32[128,8,512]{2,0,1:T(8,128)} fusion(f32[128,512]{1,0:T(8,128)S(1)} %copy-done.4, f32[5,8,8,512]{3,2,1,0:T(8,128)S(1)} %bitcast.196, f32[128,83]{0,1:T(8,128)S(1)} %bitcast.225), kind=kOutput, calls=%fused_computation.10 | convolution fusion | flops 252182528 | bytes 3035136 | tf_op jit(solution)/shard_map/dot_general | solution.py:210
  114.4 1.9 %copy.187 = f32[128,8,512]{0,2,1:T(8,128)S(1)} copy(f32[128,8,512]{2,0,1:T(8,128)} %convolution_multiply_fusion.5) | data formatting | bytes 4194304 | tf_op jit(solution)/shard_map/mul | solution.py:217
  116.3 3.6 %fusion.1 = f32[40,4096]{1,0:T(8,128)S(1)} fusion(f32[40,4096]{1,0:T(8,128)} %fusion.131, f32[40,4096]{1,0:T(8,128)} %fusion.114, f32[128,4096]{0,1:T(8,128)S(1)} %bitcast.197, f32[128,83]{0,1:T(8,128)S(1)} %bitcast.226), kind=kOutput, calls=%fused_computation.3 | convolution fusion | flops 251985920 | bytes 4083712 | tf_op jit(solution)/shard_map/dot_general | solution.py:219
  119.9 1.3 reshape.711
  121.2 0.4 reshape.714
  121.6 1.4 copy_add_fusion
  123.0 0.3 fusion.198
  123.8 1.1 fusion.3
  125.0 0.6 stack.21
  125.7 5.1 %all-to-all-start.1 = ((f32[16,1,8,83]{3,2,1,0:T(8,128)}), f32[16,1,8,83]{3,2,1,0:T(8,128)S(1)}, u32[]{:S(2)}, u32[]{:S(2)}) async-start(f32[16,1,8,83]{3,2,1,0:T(8,128)} %stack.21), calls=%async_computation.1 | async-start | bytes 131072 | tf_op jit(solution)/shard_map/all_to_all | solution.py:187
  130.7 0.4 fusion.35
  131.3 9.2 %all-to-all-done.1 = f32[16,1,8,83]{3,2,1,0:T(8,128)S(1)} async-done(((f32[16,1,8,83]{3,2,1,0:T(8,128)}), f32[16,1,8,83]{3,2,1,0:T(8,128)S(1)}, u32[]{:S(2)}, u32[]{:S(2)}) %all-to-all-start.1) | async-done | bytes 42528 | tf_op jit(solution)/shard_map/all_to_all | solution.py:187
  140.6 1.9 %collective-permute-start.6 = (f32[1,128,83]{1,2,0:T(8,128)S(1)}, f32[1,128,83]{1,2,0:T(8,128)S(1)}, u32[]{:S(2)}, u32[]{:S(2)}) collective-permute-start(f32[1,128,83]{1,2,0:T(8,128)S(1)} %copy.198), channel_id=1, source_target_pairs={{0,16},{16,32},{32,48},{48,64},{64,80},{80,96},{96,112},{112,128},... | collective-permute-start | bytes 127496 | tf_op jit(solution)/shard_map/ppermute | solution.py:16
  142.5 8.1 %collective-permute-start.7 = (f32[1,128,83]{1,2,0:T(8,128)S(1)}, f32[1,128,83]{1,2,0:T(8,128)S(1)}, u32[]{:S(2)}, u32[]{:S(2)}) collective-permute-start(f32[1,128,83]{1,2,0:T(8,128)S(1)} %copy.198), channel_id=1, source_target_pairs={{16,0},{32,16},{48,32},{64,48},{80,64},{96,80},{112,96},{128,112},... | collective-permute-start | bytes 127496 | tf_op jit(solution)/shard_map/ppermute | solution.py:17
  150.9 0.6 collective-permute-done.7
  151.5 1.5 fusion.86
  153.1 3.2 %convolution_multiply_fusion = f32[128,8,512]{2,0,1:T(8,128)} fusion(f32[128,512]{1,0:T(8,128)S(1)} %get-tuple-element.52, f32[5,8,8,512]{3,2,1,0:T(8,128)S(1)} %bitcast.191, f32[128,83]{0,1:T(8,128)S(1)} %bitcast.228), kind=kOutput, calls=%fused_computation.5 | convolution fusion | flops 252182528 | bytes 3035136 | tf_op jit(solution)/shard_map/dot_general | solution.py:210
  156.2 1.9 %copy.207 = f32[128,8,512]{0,2,1:T(8,128)S(1)} copy(f32[128,8,512]{2,0,1:T(8,128)} %convolution_multiply_fusion) | data formatting | bytes 4194304 | tf_op jit(solution)/shard_map/mul | solution.py:217
  158.2 3.9 %fusion.128 = f32[40,4096]{1,0:T(8,128)} fusion(f32[128,4096]{0,1:T(8,128)S(1)} %bitcast.201, f32[128,83]{0,1:T(8,128)} %bitcast.229), kind=kOutput, calls=%fused_computation.187 | convolution fusion | flops 251658240 | bytes 2772992 | tf_op jit(solution)/shard_map/dot_general | solution.py:219
  162.1 3.1 %convolution_multiply_fusion.1 = f32[128,8,512]{2,0,1:T(8,128)} fusion(f32[128,512]{1,0:T(8,128)S(1)} %copy-done.5, f32[5,8,8,512]{3,2,1,0:T(8,128)S(1)} %bitcast.192, f32[128,83]{1,0:T(8,128)S(1)} %bitcast.206), kind=kOutput, calls=%fused_computation.6 | convolution fusion | flops 252182528 | bytes 3057152 | tf_op jit(solution)/shard_map/dot_general | solution.py:210
  165.2 1.9 %copy.204 = f32[128,8,512]{0,2,1:T(8,128)S(1)} copy(f32[128,8,512]{2,0,1:T(8,128)} %convolution_multiply_fusion.1) | data formatting | bytes 4194304 | tf_op jit(solution)/shard_map/mul | solution.py:217
  167.1 3.2 %fusion.112 = f32[40,4096]{1,0:T(8,128)} fusion(f32[128,4096]{0,1:T(8,128)S(1)} %bitcast.202, f32[128,83]{1,0:T(8,128)S(1)} %bitcast.207), kind=kOutput, calls=%fused_computation.170 | convolution fusion | flops 251658240 | bytes 2795008 | tf_op jit(solution)/shard_map/dot_general | solution.py:219
  170.3 3.2 %convolution_multiply_fusion.2 = f32[128,8,512]{2,0,1:T(8,128)} fusion(f32[128,512]{1,0:T(8,128)S(1)} %copy-done.3, f32[5,8,8,512]{3,2,1,0:T(8,128)S(1)} %bitcast.193, f32[128,83]{0,1:T(8,128)S(1)} %bitcast.222), kind=kOutput, calls=%fused_computation.7 | convolution fusion | flops 252182528 | bytes 3035136 | tf_op jit(solution)/shard_map/dot_general | solution.py:210
  173.5 1.9 %copy.201 = f32[128,8,512]{0,2,1:T(8,128)S(1)} copy(f32[128,8,512]{2,0,1:T(8,128)} %convolution_multiply_fusion.2) | data formatting | bytes 4194304 | tf_op jit(solution)/shard_map/mul | solution.py:217
  175.4 3.6 %fusion = f32[40,4096]{1,0:T(8,128)S(1)} fusion(f32[40,4096]{1,0:T(8,128)} %fusion.128, f32[40,4096]{1,0:T(8,128)} %fusion.112, f32[128,4096]{0,1:T(8,128)S(1)} %bitcast.198, f32[128,83]{0,1:T(8,128)S(1)} %bitcast.223), kind=kOutput, calls=%fused_computation.1 | convolution fusion | flops 251985920 | bytes 4083712 | tf_op jit(solution)/shard_map/dot_general | solution.py:219
  178.9 0.4 reshape.718
  179.4 1.0 multiply_add_fusion.2
  (112 shorter events, 5.3 us)
Async XLA Ops:
  0.0 22.6 %copy-start = (f32[40,8,4,128]{3,2,1,0:T(4,128)S(1)}, f32[40,8,4,128]{3,2,1,0:T(4,128)}, u32[]{:S(2)}) copy-start(f32[40,8,4,128]{3,2,1,0:T(4,128)} %param.12) | copy-start | bytes 1966084
  0.0 19.1 %copy-start.10 = (s32[2,1024]{1,0:T(2,128)S(1)}, s32[2,1024]{1,0:T(2,128)}, u32[]{:S(2)}) copy-start(s32[2,1024]{1,0:T(2,128)} %param.19) | copy-start | bytes 24580
  0.0 22.0 %copy-start.19 = (f32[2,1024]{1,0:T(2,128)S(1)}, f32[2,1024]{1,0:T(2,128)}, u32[]{:S(2)}) copy-start(f32[2,1024]{1,0:T(2,128)} %param.20) | copy-start | bytes 24580
  1.8 20.8 %copy-start.16 = (s32[4,128]{1,0:T(4,128)S(1)}, s32[4,128]{1,0:T(4,128)}, u32[]{:S(2)}) copy-start(s32[4,128]{1,0:T(4,128)} %param.18) | copy-start | bytes 6148
  2.2 21.1 %collective-permute-start.1 = (f32[40,8,4,2]{0,1,3,2:T(8,128)S(1)}, f32[40,8,4,2]{0,1,3,2:T(8,128)S(1)}, u32[]{:S(2)}, u32[]{:S(2)}) collective-permute-start(f32[40,8,4,2]{0,1,3,2:T(8,128)S(1)} %copy.209), channel_id=1, source_target_pairs={{16,0},{32,16},{48,32},{64,48},{80,64},{96,80},{112,96},{128,112},... | collective-permute-start | bytes 30728 | tf_op jit(solution)/shard_map/ppermute | solution.py:17
  17.2 8.6 %collective-permute-start = (f32[40,8,4,2]{0,1,3,2:T(8,128)S(1)}, f32[40,8,4,2]{0,1,3,2:T(8,128)S(1)}, u32[]{:S(2)}, u32[]{:S(2)}) collective-permute-start(f32[40,8,4,2]{0,1,3,2:T(8,128)S(1)} %copy.208), channel_id=1, source_target_pairs={{0,16},{16,32},{32,48},{48,64},{64,80},{80,96},{96,112},{112,128},... | collective-permute-start | bytes 30728 | tf_op jit(solution)/shard_map/ppermute | solution.py:16
  21.3 0.8 copy-start.17
  27.0 9.7 %copy-start.12 = (f32[2,4,128]{2,1,0:T(4,128)S(1)}, f32[2,4,128]{2,1,0:T(4,128)}, u32[]{:S(2)}) copy-start(f32[2,4,128]{2,1,0:T(4,128)} %param.14) | copy-start | bytes 12292
  27.0 9.7 %copy-start.13 = (f32[2,4,128]{2,1,0:T(4,128)S(1)}, f32[2,4,128]{2,1,0:T(4,128)}, u32[]{:S(2)}) copy-start(f32[2,4,128]{2,1,0:T(4,128)} %param.13) | copy-start | bytes 12292
  27.1 30.1 %collective-permute-start.3 = (f32[40,8,2,132]{3,1,2,0:T(8,128)S(1)}, f32[40,8,2,132]{3,1,2,0:T(8,128)S(1)}, u32[]{:S(2)}, u32[]{:S(2)}) collective-permute-start(f32[40,8,2,132]{3,1,2,0:T(8,128)S(1)} %get-tuple-element.30), channel_id=1, source_target_pairs={{1,0},{2,1},{3,2},{4,3},{5,4},{6,5},{7,6},{8,7},{9,8},{10,9},{11,1... | collective-permute-start | bytes 1013768 | tf_op jit(solution)/shard_map/ppermute | solution.py:17
  31.1 26.4 %collective-permute-start.2 = (f32[40,8,2,132]{3,1,2,0:T(8,128)S(1)}, f32[40,8,2,132]{3,1,2,0:T(8,128)S(1)}, u32[]{:S(2)}, u32[]{:S(2)}) collective-permute-start(f32[40,8,2,132]{3,1,2,0:T(8,128)S(1)} %get-tuple-element.29), channel_id=1, source_target_pairs={{0,1},{1,2},{2,3},{3,4},{4,5},{5,6},{6,7},{7,8},{8,9},{9,10},{10,1... | collective-permute-start | bytes 1013768 | tf_op jit(solution)/shard_map/ppermute | solution.py:16
  58.0 0.7 copy-start.14
  58.0 0.9 copy-start.11
  58.6 0.7 copy-start.15
  59.3 2.2 %copy-start.20 = (f32[2,1024]{1,0:T(2,128)S(1)}, f32[2,1024]{1,0:T(2,128)}, u32[]{:S(2)}) copy-start(f32[2,1024]{1,0:T(2,128)} %param.21) | copy-start | bytes 24580
  59.3 2.5 %copy-start.7 = (f32[2,1024,40]{1,2,0:T(8,128)S(1)}, f32[2,1024,40]{1,2,0:T(8,128)}, u32[]{:S(2)}) copy-start(f32[2,1024,40]{1,2,0:T(8,128)} %param.22) | copy-start | bytes 983044
  62.8 14.9 %all-to-all-start = ((f32[16,1,8,83]{3,2,1,0:T(8,128)}), f32[16,1,8,83]{3,2,1,0:T(8,128)S(1)}, u32[]{:S(2)}, u32[]{:S(2)}) async-start(f32[16,1,8,83]{3,2,1,0:T(8,128)} %stack.20), calls=%async_computation | async-start | bytes 131072 | tf_op jit(solution)/shard_map/all_to_all | solution.py:187
  68.1 25.8 %copy-start.1 = (f32[40,4096]{1,0:T(8,128)}, f32[40,4096]{1,0:T(8,128)S(1)}, u32[]{:S(2)}) copy-start(f32[40,4096]{1,0:T(8,128)S(1)} %reshape.707) | copy-start | bytes 1966084
  77.7 13.9 %collective-permute-start.4 = (f32[1,128,83]{1,2,0:T(8,128)S(1)}, f32[1,128,83]{1,2,0:T(8,128)S(1)}, u32[]{:S(2)}, u32[]{:S(2)}) collective-permute-start(f32[1,128,83]{1,2,0:T(8,128)S(1)} %copy.184), channel_id=1, source_target_pairs={{0,16},{16,32},{32,48},{48,64},{64,80},{80,96},{96,112},{112,128},... | collective-permute-start | bytes 127496 | tf_op jit(solution)/shard_map/ppermute | solution.py:16
  84.1 8.4 %collective-permute-start.5 = (f32[1,128,83]{1,2,0:T(8,128)S(1)}, f32[1,128,83]{1,2,0:T(8,128)S(1)}, u32[]{:S(2)}, u32[]{:S(2)}) collective-permute-start(f32[1,128,83]{1,2,0:T(8,128)S(1)} %copy.184), channel_id=1, source_target_pairs={{16,0},{32,16},{48,32},{64,48},{80,64},{96,80},{112,96},{128,112},... | collective-permute-start | bytes 127496 | tf_op jit(solution)/shard_map/ppermute | solution.py:17
  92.4 1.5 copy-start.9
  99.1 3.9 %copy-start.6 = (f32[128,512]{1,0:T(8,128)S(1)}, f32[128,512]{1,0:T(8,128)}, u32[]{:S(2)}) copy-start(f32[128,512]{1,0:T(8,128)} %get-tuple-element.56) | copy-start | bytes 786436
  108.0 3.2 %copy-start.4 = (f32[128,512]{1,0:T(8,128)S(1)}, f32[128,512]{1,0:T(8,128)}, u32[]{:S(2)}) copy-start(f32[128,512]{1,0:T(8,128)} %get-tuple-element.55) | copy-start | bytes 786436
  119.9 3.2 %copy-start.22 = (pred[8]{0:T(512)(128)(4,1)S(1)}, pred[8]{0:T(512)(128)(4,1)}, u32[]{:S(2)}) copy-start(pred[8]{0:T(512)(128)(4,1)} %broadcast_compare_fusion) | copy-start | bytes 28
  121.2 2.4 %copy-start.18 = (f32[8]{0:T(128)S(1)}, f32[8]{0:T(128)}, u32[]{:S(2)}) copy-start(f32[8]{0:T(128)} %copy-done.17) | copy-start | bytes 100
  121.2 2.4 %copy-start.21 = (f32[2,1024]{1,0:T(2,128)S(1)}, f32[2,1024]{1,0:T(2,128)}, u32[]{:S(2)}) copy-start(f32[2,1024]{1,0:T(2,128)} %param.21) | copy-start | bytes 24580
  121.6 9.6 %copy-start.2 = (f32[40,4096]{1,0:T(8,128)S(1)}, f32[40,4096]{1,0:T(8,128)}, u32[]{:S(2)}) copy-start(f32[40,4096]{1,0:T(8,128)} %copy-done.1) | copy-start | bytes 1966084
  125.7 14.8 %all-to-all-start.1 = ((f32[16,1,8,83]{3,2,1,0:T(8,128)}), f32[16,1,8,83]{3,2,1,0:T(8,128)S(1)}, u32[]{:S(2)}, u32[]{:S(2)}) async-start(f32[16,1,8,83]{3,2,1,0:T(8,128)} %stack.21), calls=%async_computation.1 | async-start | bytes 131072 | tf_op jit(solution)/shard_map/all_to_all | solution.py:187
  140.6 10.3 %collective-permute-start.6 = (f32[1,128,83]{1,2,0:T(8,128)S(1)}, f32[1,128,83]{1,2,0:T(8,128)S(1)}, u32[]{:S(2)}, u32[]{:S(2)}) collective-permute-start(f32[1,128,83]{1,2,0:T(8,128)S(1)} %copy.198), channel_id=1, source_target_pairs={{0,16},{16,32},{32,48},{48,64},{64,80},{80,96},{96,112},{112,128},... | collective-permute-start | bytes 127496 | tf_op jit(solution)/shard_map/ppermute | solution.py:16
  142.5 9.0 %collective-permute-start.7 = (f32[1,128,83]{1,2,0:T(8,128)S(1)}, f32[1,128,83]{1,2,0:T(8,128)S(1)}, u32[]{:S(2)}, u32[]{:S(2)}) collective-permute-start(f32[1,128,83]{1,2,0:T(8,128)S(1)} %copy.198), channel_id=1, source_target_pairs={{16,0},{32,16},{48,32},{64,48},{80,64},{96,80},{112,96},{128,112},... | collective-permute-start | bytes 127496 | tf_op jit(solution)/shard_map/ppermute | solution.py:17
  151.5 1.5 copy-start.8
  158.2 3.9 %copy-start.5 = (f32[128,512]{1,0:T(8,128)S(1)}, f32[128,512]{1,0:T(8,128)}, u32[]{:S(2)}) copy-start(f32[128,512]{1,0:T(8,128)} %get-tuple-element.51) | copy-start | bytes 786436
  167.1 3.2 %copy-start.3 = (f32[128,512]{1,0:T(8,128)S(1)}, f32[128,512]{1,0:T(8,128)}, u32[]{:S(2)}) copy-start(f32[128,512]{1,0:T(8,128)} %get-tuple-element.50) | copy-start | bytes 786436
